TPU v7x, 32 devices: a whole 2x2x4 slice. The times are simulated.
32 devices in a mesh: grp: 4 (over y, core), dp: 8 (over z, x).
Axes of the slice: x: 2, y: 2, z: 4, core: 2. Of those that a mesh axis runs over, the one named last changes fastest.
Arguments:
- queries: bfloat16 [8, 4, 128, 2048], P('dp', 'grp'), may hold values from -18 to 18
- mem_keys: bfloat16 [8, 4, 256, 2048], P('dp', 'grp'), may hold values from -18 to 18
- mem_values: bfloat16 [8, 4, 256, 2048], P('dp', 'grp'), may hold values from -48 to 48
- lengths: int32 [8, 4], P('dp'), may hold values from 128 to 256, as said below
- mates: int32 [8, 4, 4], P('dp'), may hold values 0 or 1
- out_grad: bfloat16 [8, 4, 128, 2048], P('dp', 'grp'), may hold values from -6 to 6
- mlp_input: bfloat16 [8, 4, 128, 4096], P('dp', 'grp'), may hold values from -6 to 6
- gate_pre: bfloat16 [8, 4, 128, 5632], P('dp', 'grp'), may hold values from -6 to 6
- hidden_grad: bfloat16 [8, 4, 128, 5632], P('dp', 'grp'), may hold values from -0.09375 to 0.09375
Outputs:
- attn_out: bfloat16 [8, 4, 128, 2048], P('dp', 'grp')
- q_grad: bfloat16 [8, 4, 128, 2048], P('dp', 'grp')
- up_grad: float32 [4096, 5632], P(None, ('grp', 'dp'))
Inputs may be any that keep to these rules, and one draw needn't show every extreme that they name: `lengths`: each is a multiple of 128; in every group some document has 256. `mates`: A document reads its own previous context whatever its diagonal entry.
All inputs are finite; a program needn't handle non-finite values. No bound on the sum of `mates` on one device may be relied on, other than what follows from the above.
Results may differ from a plain program's by a relative error of at most 0.025.
Values may be sent and summed in bfloat16 or wider, within the bound.
A program may use at most 128 MiB of HBM per device.

v0:
```python
import math

import jax
import jax.numpy as jnp
from jax import lax
from jax.sharding import PartitionSpec as P

HEAD_DIM = 128


def head_pass(query_head, key_head, value_head, grad_head, key_mask):
    inv_root = 1.0 / math.sqrt(query_head.shape[1])
    scores = jnp.dot(query_head, key_head.T, preferred_element_type=jnp.float32) * inv_root
    scores = jnp.where(key_mask, scores, -1e30)
    highest = jnp.max(scores, axis=1, keepdims=True)
    weights = jnp.exp(scores - highest)
    row_total = jnp.sum(weights, axis=1, keepdims=True)
    weights_bf = (weights / row_total).astype(jnp.bfloat16)
    result = jnp.dot(weights_bf, value_head, preferred_element_type=jnp.float32).astype(
        jnp.bfloat16
    )
    grad_weights = jnp.dot(grad_head, value_head.T, preferred_element_type=jnp.float32)
    row_dot = jnp.sum(
        grad_head.astype(jnp.float32) * result.astype(jnp.float32), axis=1, keepdims=True
    )
    grad_scores = (weights_bf.astype(jnp.float32) * (grad_weights - row_dot)).astype(jnp.bfloat16)
    grad_query = (
        jnp.dot(grad_scores, key_head, preferred_element_type=jnp.float32) * inv_root
    ).astype(jnp.bfloat16)
    return (result, grad_query)


def per_device(
    queries, mem_keys, mem_values, lengths, mates, out_grad, mlp_input, gate_pre, hidden_grad
):
    members = lax.axis_size("grp")
    rows_q = queries.shape[2]
    mem_rows = mem_keys.shape[2]
    heads_all = queries.shape[3] // HEAD_DIM
    local_heads = heads_all // members
    docs_block = max(1, min(members, 512 // rows_q))
    block_count = members // docs_block
    row_count = docs_block * rows_q
    allowed = (mates[0] > 0) | jnp.eye(members, dtype=bool)
    live_keys = jnp.arange(mem_rows, dtype=jnp.int32)[None, :] < lengths[0][:, None]

    def split_heads(block):
        return block[0, 0].reshape(block.shape[2], members, local_heads, HEAD_DIM)

    def per_head(pieces):
        query_head, key_head, value_head, grad_head = pieces

        def block_step(block_num):
            first_row = block_num * row_count
            query_rows = lax.dynamic_slice_in_dim(query_head, first_row, row_count, 0)
            grad_rows = lax.dynamic_slice_in_dim(grad_head, first_row, row_count, 0)
            allowed_rows = lax.dynamic_slice_in_dim(allowed, block_num * docs_block, docs_block, 0)
            key_mask = jnp.broadcast_to(
                allowed_rows[:, None, :, None] & live_keys[None, None, :, :],
                (docs_block, rows_q, members, mem_rows),
            )
            key_mask = key_mask.reshape(row_count, members * mem_rows)
            return head_pass(query_rows, key_head, value_head, grad_rows, key_mask)

        results, gradients = lax.map(block_step, jnp.arange(block_count))
        return (
            results.reshape(members * rows_q, HEAD_DIM),
            gradients.reshape(members * rows_q, HEAD_DIM),
        )

    exchanged = (
        lax.all_to_all(split_heads(queries), "grp", split_axis=1, concat_axis=0, tiled=True),
        lax.all_to_all(split_heads(mem_keys), "grp", split_axis=1, concat_axis=0, tiled=True),
        lax.all_to_all(split_heads(mem_values), "grp", split_axis=1, concat_axis=0, tiled=True),
        lax.all_to_all(split_heads(out_grad), "grp", split_axis=1, concat_axis=0, tiled=True),
    )
    query_all, key_all, value_all, grad_all = [
        jnp.moveaxis(member[:, 0], 1, 0) for member in exchanged
    ]
    results, gradients = lax.map(per_head, (query_all, key_all, value_all, grad_all))
    heads_out = jnp.moveaxis(results, 0, 1)[:, None]
    heads_grad = jnp.moveaxis(gradients, 0, 1)[:, None]
    back_out, back_grad = (
        lax.all_to_all(heads_out, "grp", split_axis=0, concat_axis=1, tiled=True),
        lax.all_to_all(heads_grad, "grp", split_axis=0, concat_axis=1, tiled=True),
    )
    attn_out = back_out.reshape(1, 1, rows_q, heads_all * HEAD_DIM)
    q_grad = back_grad.reshape(1, 1, rows_q, heads_all * HEAD_DIM)
    up_cot = (
        hidden_grad[0, 0].astype(jnp.float32) * jax.nn.silu(gate_pre[0, 0].astype(jnp.float32))
    ).astype(jnp.bfloat16)
    tokens = mlp_input[0, 0]
    contract = (((0,), (0,)), ((), ()))
    slices = lax.all_to_all(up_cot, "grp", split_axis=1, concat_axis=0, tiled=True)
    partial_value = lax.dot_general(
        lax.all_gather(tokens, "grp", axis=0, tiled=True),
        slices,
        contract,
        preferred_element_type=jnp.float32,
    )
    up_grad = lax.psum_scatter(
        partial_value.astype(jnp.bfloat16), "dp", scatter_dimension=1, tiled=True
    ).astype(jnp.float32)
    return (attn_out, q_grad, up_grad)


def solution(mesh):
    return jax.shard_map(
        per_device,
        mesh=mesh,
        in_specs=(
            P("dp", "grp", None, None),
            P("dp", "grp", None, None),
            P("dp", "grp", None, None),
            P("dp", None),
            P("dp", None, None),
            P("dp", "grp", None, None),
            P("dp", "grp", None, None),
            P("dp", "grp", None, None),
            P("dp", "grp", None, None),
        ),
        out_specs=(P("dp", "grp", None, None), P("dp", "grp", None, None), P(None, ("grp", "dp"))),
        check_vma=False,
    )
```

profile of v0, /device:TPU:0, one launch (start us, length us, event | category | flops | bytes accessed | tf_op | source)
XLA Modules:
  0.0 274.2 jit_solution(2617931373299652336)
XLA Ops:
  7.9 1.8 copy.63
  9.8 1.8 copy.62
  12.5 35.7 %all_to_all.106 = bf16[128,4,1408]{0,2,1:T(8,128)(2,1)S(1)} all-to-all(bf16[128,4,1408]{0,2,1:T(8,128)(2,1)S(1)} %fusion.33), channel_id=1, replica_groups=mesh['grp'=4,'dp'=8] {'grp'}, dimensions={1} | all-to-all | bytes 2883584 | tf_op jit(solution)/shard_map/all_to_all | solution.py:94
  49.0 10.2 %all-gather.3.cloned.1.call-done = bf16[1,1,512,4096]{3,2,1,0:T(8,128)(2,1)} async-done(((bf16[1,1,128,4096]{3,2,1,0:T(8,128)(2,1)}), bf16[1,1,512,4096]{3,2,1,0:T(8,128)(2,1)}) %all-gather.3.cloned.1.call-update) | async-done | bytes 4194320 | tf_op jit(solution)/shard_map/all_gather | solution.py:96
  59.3 11.5 %fusion.27 = bf16[4096,1408]{0,1:T(8,128)(2,1)} fusion(bf16[512,1408]{1,0:T(8,128)(2,1)S(1)} %bitcast.136, bf16[1,1,512,4096]{3,2,1,0:T(8,128)(2,1)} %all-gather.3.cloned.1.call-done), kind=kOutput, calls=%fused_computation.33 | convolution fusion | flops 5911347200 | bytes 17170432 | tf_op jit(solution)/shard_map/dot_general | solution.py:95
  73.1 3.5 %all-to-all-start = ((bf16[128,4,4,128]{3,0,2,1:T(8,128)(2,1)}), bf16[128,4,4,128]{3,0,2,1:T(8,128)(2,1)S(1)}, u32[]{:S(2)}, u32[]{:S(2)}) async-start(bf16[128,4,4,128]{3,0,2,1:T(8,128)(2,1)} %copy.46), calls=%async_computation | async-start | bytes 1048576 | tf_op jit(solution)/shard_map/all_to_all | solution.py:72
  77.6 7.8 %all-to-all-done = bf16[128,4,4,128]{3,0,2,1:T(8,128)(2,1)S(1)} async-done(((bf16[128,4,4,128]{3,0,2,1:T(8,128)(2,1)}), bf16[128,4,4,128]{3,0,2,1:T(8,128)(2,1)S(1)}, u32[]{:S(2)}, u32[]{:S(2)}) %all-to-all-start) | async-done | bytes 524320 | tf_op jit(solution)/shard_map/all_to_all | solution.py:72
  86.2 3.5 %all-to-all-start.3 = ((bf16[128,4,4,128]{0,3,2,1:T(8,128)(2,1)}), bf16[128,4,4,128]{0,3,2,1:T(8,128)(2,1)S(1)}, u32[]{:S(2)}, u32[]{:S(2)}) async-start(bf16[128,4,4,128]{0,3,2,1:T(8,128)(2,1)} %bitcast.16), calls=%async_computation.3 | async-start | bytes 1048576 | tf_op jit(solution)/shard_map/all_to_all | solution.py:75
  90.2 1.3 copy.49
  91.5 6.9 %all-to-all-done.3 = bf16[128,4,4,128]{0,3,2,1:T(8,128)(2,1)S(1)} async-done(((bf16[128,4,4,128]{0,3,2,1:T(8,128)(2,1)}), bf16[128,4,4,128]{0,3,2,1:T(8,128)(2,1)S(1)}, u32[]{:S(2)}, u32[]{:S(2)}) %all-to-all-start.3) | async-done | bytes 524320 | tf_op jit(solution)/shard_map/all_to_all | solution.py:75
  99.3 3.5 %all-to-all-start.1 = ((bf16[256,4,4,128]{3,0,2,1:T(8,128)(2,1)}), bf16[256,4,4,128]{3,0,2,1:T(8,128)(2,1)S(1)}, u32[]{:S(2)}, u32[]{:S(2)}) async-start(bf16[256,4,4,128]{3,0,2,1:T(8,128)(2,1)} %copy.49), calls=%async_computation.1 | async-start | bytes 2097152 | tf_op jit(solution)/shard_map/all_to_all | solution.py:73
  103.3 1.3 copy.52
  104.7 12.5 %all-to-all-done.1 = bf16[256,4,4,128]{3,0,2,1:T(8,128)(2,1)S(1)} async-done(((bf16[256,4,4,128]{3,0,2,1:T(8,128)(2,1)}), bf16[256,4,4,128]{3,0,2,1:T(8,128)(2,1)S(1)}, u32[]{:S(2)}, u32[]{:S(2)}) %all-to-all-start.1) | async-done | bytes 1048608 | tf_op jit(solution)/shard_map/all_to_all | solution.py:73
  117.2 3.5 %all-to-all-start.2 = ((bf16[256,4,4,128]{3,0,2,1:T(8,128)(2,1)}), bf16[256,4,4,128]{3,0,2,1:T(8,128)(2,1)S(1)}, u32[]{:S(2)}, u32[]{:S(2)}) async-start(bf16[256,4,4,128]{3,0,2,1:T(8,128)(2,1)} %copy.52), calls=%async_computation.2 | async-start | bytes 2097152 | tf_op jit(solution)/shard_map/all_to_all | solution.py:74
  122.7 12.4 %all-to-all-done.2 = bf16[256,4,4,128]{3,0,2,1:T(8,128)(2,1)S(1)} async-done(((bf16[256,4,4,128]{3,0,2,1:T(8,128)(2,1)}), bf16[256,4,4,128]{3,0,2,1:T(8,128)(2,1)S(1)}, u32[]{:S(2)}, u32[]{:S(2)}) %all-to-all-start.2) | async-done | bytes 1048608 | tf_op jit(solution)/shard_map/all_to_all | solution.py:74
  135.2 31.1 %while.13 = (s32[]{:T(128)}, bf16[4,512,128]{1,2,0:T(8,128)(2,1)}, bf16[4,512,128]{2,1,0:T(8,128)(2,1)}, pred[4,4]{1,0:T(4,128)(4,1)S(1)}, bf16[4,512,128]{2,1,0...) while((s32[]{:T(128)}, bf16[4,512,128]{1,2,0:T(8,128)(2,1)}, ...), condition=%wide.region_4.5_spmd.clone, body=%wide.region_0.4_spmd.clone.sunk | while | flops 543624704 | bytes 14053521 | solution.py:80
  137.0 1.5 fusion.49
  140.6 2.4 fusion.51
  144.7 1.5 fusion.49
  148.4 2.4 fusion.51
  152.5 1.5 fusion.49
  156.2 2.4 fusion.51
  160.3 1.5 fusion.49
  163.9 2.4 fusion.51
  166.3 2.2 copy.68
  168.6 3.5 %all-to-all-start.5 = ((bf16[512,1,4,128]{3,2,1,0:T(4,128)(2,1)}), bf16[512,1,4,128]{3,2,1,0:T(4,128)(2,1)S(1)}, u32[]{:S(2)}, u32[]{:S(2)}) async-start(bf16[512,1,4,128]{3,2,1,0:T(4,128)(2,1)} %bitcast.100), calls=%async_computation.5 | async-start | bytes 1048576 | tf_op jit(solution)/shard_map/all_to_all | solution.py:85
  172.0 2.1 copy.58
  174.2 6.7 %all-to-all-done.5 = bf16[512,1,4,128]{3,2,1,0:T(4,128)(2,1)S(1)} async-done(((bf16[512,1,4,128]{3,2,1,0:T(4,128)(2,1)}), bf16[512,1,4,128]{3,2,1,0:T(4,128)(2,1)S(1)}, u32[]{:S(2)}, u32[]{:S(2)}) %all-to-all-start.5) | async-done | bytes 524320 | tf_op jit(solution)/shard_map/all_to_all | solution.py:85
  180.8 3.5 %all-to-all-start.4 = ((bf16[512,1,4,128]{3,2,1,0:T(4,128)(2,1)}), bf16[512,1,4,128]{3,2,1,0:T(4,128)(2,1)S(1)}, u32[]{:S(2)}, u32[]{:S(2)}) async-start(bf16[512,1,4,128]{3,2,1,0:T(4,128)(2,1)} %bitcast.23), calls=%async_computation.4 | async-start | bytes 1048576 | tf_op jit(solution)/shard_map/all_to_all | solution.py:84
  185.7 7.4 %all-to-all-done.4 = bf16[512,1,4,128]{3,2,1,0:T(4,128)(2,1)S(1)} async-done(((bf16[512,1,4,128]{3,2,1,0:T(4,128)(2,1)}), bf16[512,1,4,128]{3,2,1,0:T(4,128)(2,1)S(1)}, u32[]{:S(2)}, u32[]{:S(2)}) %all-to-all-start.4) | async-done | bytes 524320 | tf_op jit(solution)/shard_map/all_to_all | solution.py:84
  194.5 69.7 %reduce-scatter.2.cloned.1.call-done = bf16[4096,176]{0,1:T(8,128)(2,1)} async-done(((bf16[4096,1408]{0,1:T(8,128)(2,1)}), bf16[4096,176]{0,1:T(8,128)(2,1)}) %reduce-scatter.2.cloned.1.call-update) | async-done | bytes 1441808 | tf_op jit(solution)/shard_map/reduce_scatter | solution.py:101
  264.1 3.3 %convert_element_type.62 = f32[4096,176]{0,1:T(8,128)} convert(bf16[4096,176]{0,1:T(8,128)(2,1)} %reduce-scatter.2.cloned.1.call-done) | non-fusion elementwise | flops 720896 | bytes 4325376 | tf_op jit(solution)/shard_map/convert_element_type | solution.py:103
  (82 shorter events, 28.6 us)
Async XLA Ops:
  7.2 52.1 %all-gather.3.cloned.1.call-start = ((), (), s32[]{:S(2)}) async-start(), calls=%async_computation.9 | async-start | bytes 5242880 | tf_op jit(solution)/shard_map/all_gather | solution.py:96
  7.9 256.2 %reduce-scatter.2.cloned.1.call-start = ((), (), s32[]{:S(2)}) async-start(), calls=%async_computation.8 | async-start | bytes 12976128 | tf_op jit(solution)/shard_map/reduce_scatter | solution.py:101
  70.8 1.0 copy-start.6
  71.8 4.8 %copy-start.7 = (bf16[1,1,128,2048]{3,2,1,0:T(8,128)(2,1)S(1)}, bf16[1,1,128,2048]{3,2,1,0:T(8,128)(2,1)}, u32[]{:S(2)}) copy-start(bf16[1,1,128,2048]{3,2,1,0:T(8,128)(2,1)} %param.16) | copy-start | bytes 1572868
  72.1 17.6 %copy-start.4 = (bf16[1,1,256,2048]{3,2,1,0:T(8,128)(2,1)S(1)}, bf16[1,1,256,2048]{3,2,1,0:T(8,128)(2,1)}, u32[]{:S(2)}) copy-start(bf16[1,1,256,2048]{3,2,1,0:T(8,128)(2,1)} %param.12) | copy-start | bytes 3145732
  73.1 12.3 %all-to-all-start = ((bf16[128,4,4,128]{3,0,2,1:T(8,128)(2,1)}), bf16[128,4,4,128]{3,0,2,1:T(8,128)(2,1)S(1)}, u32[]{:S(2)}, u32[]{:S(2)}) async-start(bf16[128,4,4,128]{3,0,2,1:T(8,128)(2,1)} %copy.46), calls=%async_computation | async-start | bytes 1048576 | tf_op jit(solution)/shard_map/all_to_all | solution.py:72
  85.4 0.8 copy-start
  86.2 12.3 %all-to-all-start.3 = ((bf16[128,4,4,128]{0,3,2,1:T(8,128)(2,1)}), bf16[128,4,4,128]{0,3,2,1:T(8,128)(2,1)S(1)}, u32[]{:S(2)}, u32[]{:S(2)}) async-start(bf16[128,4,4,128]{0,3,2,1:T(8,128)(2,1)} %bitcast.16), calls=%async_computation.3 | async-start | bytes 1048576 | tf_op jit(solution)/shard_map/all_to_all | solution.py:75
  90.2 12.6 %copy-start.5 = (bf16[1,1,256,2048]{3,2,1,0:T(8,128)(2,1)S(1)}, bf16[1,1,256,2048]{3,2,1,0:T(8,128)(2,1)}, u32[]{:S(2)}) copy-start(bf16[1,1,256,2048]{3,2,1,0:T(8,128)(2,1)} %param.13) | copy-start | bytes 3145732
  98.5 0.8 copy-start.2
  99.3 17.9 %all-to-all-start.1 = ((bf16[256,4,4,128]{3,0,2,1:T(8,128)(2,1)}), bf16[256,4,4,128]{3,0,2,1:T(8,128)(2,1)S(1)}, u32[]{:S(2)}, u32[]{:S(2)}) async-start(bf16[256,4,4,128]{3,0,2,1:T(8,128)(2,1)} %copy.49), calls=%async_computation.1 | async-start | bytes 2097152 | tf_op jit(solution)/shard_map/all_to_all | solution.py:73
  103.3 17.4 %copy-start.8 = (s32[1,4,4]{2,1,0:T(4,128)S(1)}, s32[1,4,4]{2,1,0:T(4,128)}, u32[]{:S(2)}) copy-start(s32[1,4,4]{2,1,0:T(4,128)} %param.15) | copy-start | bytes 196
  104.7 16.1 %copy-start.1 = (bf16[128,4,4,128]{3,0,2,1:T(8,128)(2,1)S(1)}, bf16[128,4,4,128]{3,0,2,1:T(8,128)(2,1)}, u32[]{:S(2)}) copy-start(bf16[128,4,4,128]{3,0,2,1:T(8,128)(2,1)} %copy-done) | copy-start | bytes 1572868
  104.7 16.9 %copy-start.3 = (bf16[128,4,4,128]{0,3,2,1:T(8,128)(2,1)S(1)}, bf16[128,4,4,128]{0,3,2,1:T(8,128)(2,1)}, u32[]{:S(2)}) copy-start(bf16[128,4,4,128]{0,3,2,1:T(8,128)(2,1)} %copy-done.2) | copy-start | bytes 1572868
  117.2 17.9 %all-to-all-start.2 = ((bf16[256,4,4,128]{3,0,2,1:T(8,128)(2,1)}), bf16[256,4,4,128]{3,0,2,1:T(8,128)(2,1)S(1)}, u32[]{:S(2)}, u32[]{:S(2)}) async-start(bf16[256,4,4,128]{3,0,2,1:T(8,128)(2,1)} %copy.52), calls=%async_computation.2 | async-start | bytes 2097152 | tf_op jit(solution)/shard_map/all_to_all | solution.py:74
  122.6 12.6 %copy-start.9 = (s32[1,4]{1,0:T(1,128)S(1)}, s32[1,4]{1,0:T(1,128)}, u32[]{:S(2)}) copy-start(s32[1,4]{1,0:T(1,128)} %param.14) | copy-start | bytes 52
  168.6 12.3 %all-to-all-start.5 = ((bf16[512,1,4,128]{3,2,1,0:T(4,128)(2,1)}), bf16[512,1,4,128]{3,2,1,0:T(4,128)(2,1)S(1)}, u32[]{:S(2)}, u32[]{:S(2)}) async-start(bf16[512,1,4,128]{3,2,1,0:T(4,128)(2,1)} %bitcast.100), calls=%async_computation.5 | async-start | bytes 1048576 | tf_op jit(solution)/shard_map/all_to_all | solution.py:85
  180.8 12.3 %all-to-all-start.4 = ((bf16[512,1,4,128]{3,2,1,0:T(4,128)(2,1)}), bf16[512,1,4,128]{3,2,1,0:T(4,128)(2,1)S(1)}, u32[]{:S(2)}, u32[]{:S(2)}) async-start(bf16[512,1,4,128]{3,2,1,0:T(4,128)(2,1)} %bitcast.23), calls=%async_computation.4 | async-start | bytes 1048576 | tf_op jit(solution)/shard_map/all_to_all | solution.py:84
Sparse Core Ops, SparseCore 0:
  9.5 49.6 all-gather.2
  71.0 193.1 reduce-scatter.1
where the time goes:
time: 275 us; the launch traced here: 274 us
  waiting for transfers between devices  134 us (49%)
  blocking collectives  35.7 us (13%)
  matrix products  31.7 us (12%)
  local copies, waits for them, and re-layouts  28.4 us (10%)
  starting transfers between devices  21 us (8%)
  between operations  14.3 us (5%)
  other arithmetic  8.71 us (3%)
    reduce_scatter x1, waiting for transfers between devices, per_device(): lax.psum_scatter(partial_value.astype(jnp.bfloat16), 'dp', scatter_dimens...  69.7 us
    all_to_all x1, blocking collectives, per_device(): lax.all_to_all(up_cot, 'grp', split_axis=1, concat_axis=0, tiled=True)  35.7 us
    all_to_all x1, waiting for transfers between devices, per_device(): lax.all_to_all(split_heads(mem_keys), 'grp', split_axis=1, concat_axis=0,...  12.5 us
    all_to_all x1, waiting for transfers between devices, per_device(): lax.all_to_all(split_heads(mem_values), 'grp', split_axis=1, concat_axis=...  12.4 us
    dot_general x1, matrix products, per_device(): lax.dot_general(lax.all_gather(tokens, 'grp', axis=0, tiled=True), slices...  11.5 us
    all_gather x1, waiting for transfers between devices, per_device(): lax.all_gather(tokens, 'grp', axis=0, tiled=True)  10.2 us
    dot_general x4, matrix products, head_pass(): jnp.dot(grad_scores, key_head, preferred_element_type=jnp.float32)  9.52 us
    unnamed x26, local copies, waits for them, and re-layouts  8.61 us
  transfers between devices with their start and end apart: 8, of which 8 were waited for; matrix products, arithmetic and copies ran while one was open for 19% of the time, Pallas kernels for 0%

commit v1 on v0

--- a/solution.py
+++ b/solution.py
@@ -1,8 +1,11 @@
+import functools
 import math
 
 import jax
 import jax.numpy as jnp
 from jax import lax
+from jax.experimental import pallas as pl
+from jax.experimental.pallas import tpu as pltpu
 from jax.sharding import PartitionSpec as P
 
 HEAD_DIM = 128
@@ -104,9 +107,418 @@
     return (attn_out, q_grad, up_grad)
 
 
+MESH = pl.DeviceIdType.MESH
+F32 = jnp.float32
+BF16 = jnp.bfloat16
+WIDTH = 512
+
+
+def fused_kernel(
+    nz,
+    mask_ref, q_ref, k_ref, v_ref, g_ref, x_ref, ct_ref,
+    attn_ref, qgrad_ref, up_ref,
+    xall, ctall, qb, kb, vb, gb, res, back, outgo, income,
+    x_send, x_recv, c_send, c_recv, a_send, a_recv, b_send, b_recv, z_send, z_recv,
+):
+    grp = lax.axis_index("grp")
+    dp = lax.axis_index("dp")
+    y, c = grp // 2, lax.rem(grp, 2)
+    z, x = dp // 2, lax.rem(dp, 2)
+    rows = x_ref.shape[0]
+    chunks = xall.shape[0]
+    members = qb.shape[0]
+    span = qb.shape[2]
+    heads = span // HEAD_DIM
+    mem_rows = kb.shape[1]
+    inv_root = 1.0 / math.sqrt(HEAD_DIM)
+
+    def device(zz, xx, yy, cc):
+        return {"dp": zz * 2 + xx, "grp": yy * 2 + cc}
+
+    def block(xx, yy, cc):
+        return xx * 4 + yy * 2 + cc
+
+    def peer(r):
+        px = lax.rem(x + r // 4, 2)
+        py = lax.rem(y + lax.rem(r // 2, 2), 2)
+        pc = lax.rem(c + lax.rem(r, 2), 2)
+        return px, py, pc
+
+    barrier = pltpu.get_barrier_semaphore()
+    for r in range(1, 8):
+        pl.semaphore_signal(barrier, inc=1, device_id=device(z, *peer(r)), device_id_type=MESH)
+
+    @pl.when(z > 0)
+    def _():
+        pl.semaphore_signal(barrier, inc=1, device_id=device(z - 1, x, y, c), device_id_type=MESH)
+
+    @pl.when(z < nz - 1)
+    def _():
+        pl.semaphore_signal(barrier, inc=1, device_id=device(z + 1, x, y, c), device_id_type=MESH)
+
+    mine = block(x, y, c)
+
+    def rows_of(b):
+        return pl.ds(pl.multiple_of(b * rows, rows), rows)
+
+    def cols_of(k, width):
+        return pl.ds(pl.multiple_of(k * width, width), width)
+
+    sib = device(z, x, y, 1 - c)
+    xdev = device(z, 1 - x, y, c)
+    ydev = device(z, x, 1 - y, c)
+    own_b = mine
+    x_b = block(1 - x, y, c)
+    y_b = block(x, 1 - y, c)
+    d_b = block(1 - x, 1 - y, c)
+
+    def own_copy(k, role, dev):
+        return pltpu.make_async_remote_copy(
+            src_ref=x_ref.at[:, cols_of(k, WIDTH)],
+            dst_ref=xall.at[k, rows_of(own_b)],
+            send_sem=x_send.at[k, role], recv_sem=x_recv.at[k, role],
+            device_id=dev, device_id_type=MESH,
+        )
+
+    def relay_copy(k, role, b, dev):
+        return pltpu.make_async_remote_copy(
+            src_ref=xall.at[k, rows_of(b)],
+            dst_ref=xall.at[k, rows_of(b)],
+            send_sem=x_send.at[k, role], recv_sem=x_recv.at[k, role],
+            device_id=dev, device_id_type=MESH,
+        )
+
+    def x_copies(k):
+        return [
+            own_copy(k, 0, xdev), own_copy(k, 1, ydev), relay_copy(k, 2, y_b, xdev),
+            own_copy(k, 3, sib), relay_copy(k, 4, x_b, sib), relay_copy(k, 5, y_b, sib),
+            relay_copy(k, 6, d_b, sib),
+        ]
+
+    def start_own(k):
+        cs = x_copies(k)
+        cs[1].start()
+        cs[0].start()
+        cs[3].start()
+
+    def relay(k):
+        cs = x_copies(k)
+        cs[1].wait_recv()
+        cs[2].start()
+        cs[5].start()
+        cs[0].wait_recv()
+        cs[4].start()
+        cs[2].wait_recv()
+        cs[6].start()
+
+    def ct_copy(t, r):
+        px, py, pc = peer(r)
+        return pltpu.make_async_remote_copy(
+            src_ref=ct_ref.at[py * 2 + pc, t * 2 + px],
+            dst_ref=ctall.at[t, :, rows_of(mine)],
+            send_sem=c_send.at[t, r], recv_sem=c_recv.at[t, r],
+            device_id=device(z, px, py, pc), device_id_type=MESH,
+        )
+
+    def ct_start(t):
+        @pl.loop(1, 8)
+        def _(r):
+            ct_copy(t, r).start()
+
+    def ct_wait(t):
+        @pl.loop(1, 8)
+        def _(r):
+            ct_copy(t, r).wait_recv()
+
+    half = nz // 2
+
+    def dest(i):
+        down = nz - 1 - i
+        down = jnp.where(down <= z, down - 1, down)
+        up = jnp.where(i >= z, i + 1, i)
+        return jnp.where(z < half, down, up)
+
+    def att_copy(a, src, dst, j):
+        p = lax.rem(grp + j, members)
+        return pltpu.make_async_remote_copy(
+            src_ref=src.at[:, cols_of(p, span)],
+            dst_ref=dst.at[grp],
+            send_sem=a_send.at[a, j], recv_sem=a_recv.at[a, j],
+            device_id={"dp": dp, "grp": p}, device_id_type=MESH,
+        )
+
+    pairs = ((q_ref, qb), (k_ref, kb), (v_ref, vb), (g_ref, gb))
+
+    def att_start(which):
+        for a in which:
+            for j in range(1, members):
+                att_copy(a, *pairs[a], j).start()
+
+    def back_copy(h, o, j):
+        p = lax.rem(grp + j, members)
+        return pltpu.make_async_remote_copy(
+            src_ref=res.at[h, o, p], dst_ref=back.at[h, o, grp],
+            send_sem=b_send.at[h, o, j], recv_sem=b_recv.at[h, o, j],
+            device_id={"dp": dp, "grp": p}, device_id_type=MESH,
+        )
+
+    def head(h):
+        cols = cols_of(h, HEAD_DIM)
+        nt = (((1,), (1,)), ((), ()))
+        kh = kb[:, :, cols].reshape(members * mem_rows, HEAD_DIM)
+        vh = vb[:, :, cols].reshape(members * mem_rows, HEAD_DIM)
+
+        @pl.loop(0, members)
+        def _(m):
+            qh = qb[m, :, cols]
+            gh = gb[m, :, cols]
+            s = lax.dot_general(qh, kh, nt, preferred_element_type=F32) * inv_root
+            s = jnp.where(mask_ref[m] > 0, s, -1e30)
+            w = jnp.exp(s - jnp.max(s, axis=1, keepdims=True))
+            p = (w / jnp.sum(w, axis=1, keepdims=True)).astype(BF16)
+            o = jnp.dot(p, vh, preferred_element_type=F32).astype(BF16)
+            gp = lax.dot_general(gh, vh, nt, preferred_element_type=F32)
+            rd = jnp.sum(gh.astype(F32) * o.astype(F32), axis=1, keepdims=True)
+            gs = (p.astype(F32) * (gp - rd)).astype(BF16)
+            res[h, 0, m] = o
+            res[h, 1, m] = (jnp.dot(gs, kh, preferred_element_type=F32) * inv_root).astype(BF16)
+
+        for o in range(2):
+            for j in range(1, members):
+                back_copy(h, o, j).start()
+
+    def z_copy(t, k):
+        right = t > z
+        nxt = jnp.where(right, z + 1, z - 1)
+        nxt = jnp.minimum(jnp.maximum(nxt, 0), nz - 1)
+        slot = jnp.where(jnp.logical_and(nxt == t, t < z), nz, t)
+        return pltpu.make_async_remote_copy(
+            src_ref=outgo.at[t, k], dst_ref=income.at[slot, k],
+            send_sem=z_send.at[t, k], recv_sem=z_recv.at[slot, k],
+            device_id=device(nxt, x, y, c), device_id_type=MESH,
+        )
+
+    def z_wait(slot, k):
+        pltpu.make_async_remote_copy(
+            src_ref=income.at[slot, k], dst_ref=income.at[slot, k],
+            send_sem=z_send.at[0, k], recv_sem=z_recv.at[slot, k],
+            device_id=sib, device_id_type=MESH,
+        ).wait_recv()
+
+    def part(t, k):
+        return jnp.dot(ctall[t], xall[k], preferred_element_type=F32)
+
+    def push(k):
+        @pl.loop(0, nz - 1)
+        def _(i):
+            t = dest(i)
+
+            @pl.when(k == 0)
+            def _():
+                ct_wait(t)
+
+            value = part(t, k)
+            has = jnp.where(t > z, z > 0, z < nz - 1)
+
+            @pl.when(has)
+            def _():
+                z_wait(t, k)
+                outgo[t, k] = (value + income[t, k].astype(F32)).astype(BF16)
+
+            @pl.when(jnp.logical_not(has))
+            def _():
+                outgo[t, k] = value.astype(BF16)
+
+            z_copy(t, k).start()
+
+    def finish(k):
+        cols = cols_of(k, WIDTH)
+        up_ref[:, cols] = part(z, k)
+
+        @pl.when(z > 0)
+        def _():
+            z_wait(z, k)
+            up_ref[:, cols] += income[z, k].astype(F32)
+
+        @pl.when(z < nz - 1)
+        def _():
+            z_wait(nz, k)
+            up_ref[:, cols] += income[nz, k].astype(F32)
+
+    for t in range(nz):
+        ctall[t, :, rows_of(mine)] = ct_ref[grp, t * 2 + x]
+    for k in range(chunks):
+        xall[k, rows_of(mine)] = x_ref[:, k * WIDTH : (k + 1) * WIDTH]
+    for src, dst in pairs:
+        dst[grp] = src[:, cols_of(grp, span)]
+
+    others = 7 + jnp.where(z > 0, 1, 0) + jnp.where(z < nz - 1, 1, 0)
+    pl.semaphore_wait(barrier, others)
+
+    ct_start(dest(0))
+    start_own(0)
+
+    @pl.loop(1, nz - 1)
+    def _(i):
+        ct_start(dest(i))
+
+    start_own(1)
+    ct_start(z)
+    relay(0)
+
+    first_head = 3
+    lag = 3
+
+    @pl.loop(0, chunks)
+    def _(k):
+        for role in range(3, 7):
+            x_copies(k)[role].wait_recv()
+        push(k)
+
+        @pl.when(k + 2 < chunks)
+        def _():
+            start_own(k + 2)
+
+        @pl.when(k == 0)
+        def _():
+            att_start((0, 1))
+
+        @pl.when(k == 1)
+        def _():
+            att_start((2, 3))
+
+        @pl.when(k + 1 < chunks)
+        def _():
+            relay(k + 1)
+
+        @pl.when(k == first_head)
+        def _():
+            for a in range(4):
+                for j in range(1, members):
+                    att_copy(a, *pairs[a], j).wait_recv()
+
+        @pl.when(jnp.logical_and(k >= first_head, k < first_head + heads))
+        def _():
+            head(k - first_head)
+
+        @pl.when(k == lag)
+        def _():
+            ct_wait(z)
+
+        @pl.when(k >= lag)
+        def _():
+            finish(k - lag)
+
+    @pl.loop(chunks - lag, chunks)
+    def _(k):
+        finish(k)
+
+    for o, ref in ((0, attn_ref), (1, qgrad_ref)):
+        for h in range(heads):
+            for j in range(1, members):
+                back_copy(h, o, j).wait_recv()
+                p = lax.rem(grp + members - j, members)
+                ref[:, pl.ds(pl.multiple_of(p * span + h * HEAD_DIM, HEAD_DIM), HEAD_DIM)] = back[h, o, p]
+            ref[:, pl.ds(pl.multiple_of(grp * span + h * HEAD_DIM, HEAD_DIM), HEAD_DIM)] = res[h, o, grp]
+
+    @pl.loop(0, chunks)
+    def _(k):
+        for copy in x_copies(k):
+            copy.wait_send()
+
+        @pl.loop(0, nz - 1)
+        def _(i):
+            z_copy(dest(i), k).wait_send()
+
+    @pl.loop(0, nz)
+    def _(t):
+        @pl.loop(1, 8)
+        def _(r):
+            ct_copy(t, r).wait_send()
+
+    for a in range(4):
+        for j in range(1, members):
+            att_copy(a, *pairs[a], j).wait_send()
+
+    @pl.loop(0, heads)
+    def _(h):
+        for o in range(2):
+            for j in range(1, members):
+                back_copy(h, o, j).wait_send()
+
+
+def fused_call(
+    nz, queries, mem_keys, mem_values, lengths, mates, out_grad, mlp_input, gate_pre, hidden_grad
+):
+    members = lax.axis_size("grp")
+    groups = lax.axis_size("dp")
+    rows, width = queries.shape[2:]
+    mem_rows = mem_keys.shape[2]
+    model, hidden = mlp_input.shape[3], gate_pre.shape[3]
+    span = width // members
+    heads = span // HEAD_DIM
+    own = hidden // (members * groups)
+    layer = 2 * members
+    chunks = model // WIDTH
+    up_cot = (
+        hidden_grad[0, 0].astype(F32) * jax.nn.silu(gate_pre[0, 0].astype(F32))
+    ).astype(BF16)
+    ct = up_cot.T.reshape(members, groups, own, rows)
+    allowed = (mates[0] > 0) | jnp.eye(members, dtype=bool)
+    live = jnp.arange(mem_rows, dtype=jnp.int32)[None, :] < lengths[0][:, None]
+    mask = (allowed[:, :, None] & live[None]).astype(F32).reshape(members, 1, members * mem_rows)
+    vm = pl.BlockSpec(memory_space=pltpu.VMEM)
+    dma = pltpu.SemaphoreType.DMA
+    attn, qgrad, up = pl.pallas_call(
+        functools.partial(fused_kernel, nz),
+        out_shape=(
+            jax.ShapeDtypeStruct((rows, width), BF16),
+            jax.ShapeDtypeStruct((rows, width), BF16),
+            jax.ShapeDtypeStruct((own, model), F32),
+        ),
+        in_specs=[vm] * 7,
+        out_specs=(vm, vm, vm),
+        scratch_shapes=[
+            pltpu.VMEM((chunks, layer * rows, WIDTH), BF16),
+            pltpu.VMEM((nz, own, layer * rows), BF16),
+            pltpu.VMEM((members, rows, span), BF16),
+            pltpu.VMEM((members, mem_rows, span), BF16),
+            pltpu.VMEM((members, mem_rows, span), BF16),
+            pltpu.VMEM((members, rows, span), BF16),
+            pltpu.VMEM((heads, 2, members, rows, HEAD_DIM), BF16),
+            pltpu.VMEM((heads, 2, members, rows, HEAD_DIM), BF16),
+            pltpu.VMEM((nz, chunks, own, WIDTH), BF16),
+            pltpu.VMEM((nz + 1, chunks, own, WIDTH), BF16),
+            dma((chunks, 7)), dma((chunks, 7)),
+            dma((nz, 8)), dma((nz, 8)),
+            dma((4, members)), dma((4, members)),
+            dma((heads, 2, members)), dma((heads, 2, members)),
+            dma((nz, chunks)), dma((nz + 1, chunks)),
+        ],
+        compiler_params=pltpu.CompilerParams(
+            collective_id=0, has_side_effects=True, vmem_limit_bytes=60 * 1024 * 1024
+        ),
+        name="fused",
+    )(
+        mask, queries[0, 0], mem_keys[0, 0], mem_values[0, 0], out_grad[0, 0], mlp_input[0, 0], ct
+    )
+    return attn[None, None], qgrad[None, None], up.T
+
+
+def choose(*args):
+    members, groups = lax.axis_size("grp"), lax.axis_size("dp")
+    near = 1 << ((groups.bit_length() - 1) // 2)
+    hidden, model = args[7].shape[3], args[6].shape[3]
+    own = hidden // (members * groups)
+    fits = members == 4 and near == 2 and groups % 2 == 0 and own % 16 == 0 and model % WIDTH == 0
+    if fits and model // WIDTH >= 3 + args[0].shape[3] // members // HEAD_DIM:
+        return fused_call(groups // near, *args)
+    return per_device(*args)
+
+
 def solution(mesh):
     return jax.shard_map(
-        per_device,
+        choose,
         mesh=mesh,
         in_specs=(
             P("dp", "grp", None, None),

time: 275 us -> 180 us (0.65)
  Pallas kernels: 0 us -> 165 us
  waiting for transfers between devices: 134 us -> 0 us
  blocking collectives: 35.7 us -> 0 us
  matrix products: 31.7 us -> 0 us
  starting transfers between devices: 21 us -> 0 us
  local copies, waits for them, and re-layouts: 28.4 us -> 9.82 us
  between operations: 14.3 us -> 0.65 us
  other arithmetic: 8.71 us -> 3.98 us
    pallas_call x0 -> x1, Pallas kernels: none -> 165 us  [fused_call(): pl.pallas_call(functools.partial(fused_kernel, nz), out_shape=(jax.ShapeD...]
    reduce_scatter x1 -> x0, waiting for transfers between devices: 69.7 us -> none  [per_device(): lax.psum_scatter(partial_value.astype(jnp.bfloat16), 'dp', scatter_dimens...]
    all_to_all x6 -> x0, waiting for transfers between devices: 53.7 us -> none  [the longest x1 12.5 us: per_device(): lax.all_to_all(split_heads(mem_keys), 'grp', split_axis=1, concat_axis=0,...]
    all_to_all x1 -> x0, blocking collectives: 35.7 us -> none  [per_device(): lax.all_to_all(up_cot, 'grp', split_axis=1, concat_axis=0, tiled=True)]
    dot_general x13 -> x0, matrix products: 31.7 us -> none  [the longest x1 11.5 us: per_device(): lax.dot_general(lax.all_gather(tokens, 'grp', axis=0, tiled=True), slices...]
    all_to_all x6 -> x0, starting transfers between devices: 20.9 us -> none  [the longest x1 3.52 us: per_device(): lax.all_to_all(split_heads(mem_keys), 'grp', split_axis=1, concat_axis=0,...]
    all_gather x1 -> x0, waiting for transfers between devices: 10.2 us -> none  [per_device(): lax.all_gather(tokens, 'grp', axis=0, tiled=True)]
    while x6 -> x0, local copies, waits for them, and re-layouts: 5.39 us -> none  [the longest x2 4.35 us: per_device(): lax.map(per_head, (query_all, key_all, value_all, grad_all))]
  transfers between devices with their start and end apart: 8 -> 0, of which waited for: 8 -> 0; matrix products, arithmetic and copies ran while one was open for 19% -> 0% of each run, Pallas kernels for 0% -> 0%
where the time goes in v1:
time: 180 us; the launch traced here: 179 us
  Pallas kernels  165 us (92%)
  local copies, waits for them, and re-layouts  9.82 us (5%)
  other arithmetic  3.98 us (2%)
    pallas_call x1, Pallas kernels, fused_call(): pl.pallas_call(functools.partial(fused_kernel, nz), out_shape=(jax.ShapeD...  165 us
    unnamed x5, local copies, waits for them, and re-layouts  7.47 us

profile of v1, /device:TPU:0, one launch (start us, length us, event | category | flops | bytes accessed | tf_op | source)
XLA Modules:
  0.0 179.3 jit_solution(14999449957406272334)
XLA Ops:
  0.6 0.7 fusion.6
  1.3 0.1 and.22
  1.4 0.7 lt.23
  2.2 0.6 and_convert_fusion.mask_ref
  2.8 2.7 %fusion.5 = bf16[5632,128]{0,1:T(8,128)(2,1)S(1)} fusion(bf16[1,1,128,5632]{3,2,1,0:T(8,128)(2,1)} %param.16, bf16[1,1,128,5632]{3,2,1,0:T(8,128)(2,1)} %param.17), kind=kLoop, calls=%fused_computation.7 | loop fusion | flops 5767168 | bytes 4325376 | tf_op jit(solution)/shard_map/transpose | solution.py:466
  5.5 1.5 copy.14
  7.0 164.8 %fused.1 = (bf16[128,2048]{1,0:T(8,128)(2,1)}, bf16[128,2048]{1,0:T(8,128)(2,1)}, f32[176,4096]{1,0:T(8,128)}) custom-call(f32[4,1,1024]{2,1,0:T(1,128)} %and_convert_fusion.mask_ref, bf16[128,2048]{1,0:T(8,128)(2,1)} %bitcast.35, bf16[256,2048]{1,0:T(8,128)(2,1)} %bitcast.30, bf16[256,2048]{1,0:T(8,128)(2,1)} %bitcast.31, bf16[128,2048]{1,0:T(8,128)(2,1)} %bitcast.36, ...), custom_call_target="tpu_custom_call" | custom-call | tf_op jit(solution)/shard_map/fused/pallas_call | solution.py:472
  171.8 1.9 %copy.19 = bf16[1,1,128,2048]{3,2,1,0:T(8,128)(2,1)} copy(bf16[1,1,128,2048]{3,2,1,0:T(8,128)(2,1)} %bitcast.34) | data formatting | bytes 1048576
  173.7 1.9 %copy.20 = bf16[1,1,128,2048]{3,2,1,0:T(8,128)(2,1)} copy(bf16[1,1,128,2048]{3,2,1,0:T(8,128)(2,1)} %bitcast.33) | data formatting | bytes 1048576
  175.6 3.7 %copy.21 = f32[4096,176]{0,1:T(8,128)} copy(f32[4096,176]{0,1:T(8,128)} %bitcast.29) | data formatting | bytes 5767168
  (4 shorter events, 0.0 us)

commit v2 on v1

--- a/solution.py
+++ b/solution.py
@@ -201,13 +201,16 @@
         cs[0].start()
         cs[3].start()
 
-    def relay(k):
+    def relay_far(k):
         cs = x_copies(k)
         cs[1].wait_recv()
         cs[2].start()
         cs[5].start()
         cs[0].wait_recv()
         cs[4].start()
+
+    def relay_near(k):
+        cs = x_copies(k)
         cs[2].wait_recv()
         cs[6].start()
 
@@ -357,16 +360,19 @@
 
     ct_start(dest(0))
     start_own(0)
-
-    @pl.loop(1, nz - 1)
+    ct_start(dest(1))
+    relay_far(0)
+    start_own(1)
+
+    @pl.loop(2, nz - 1)
     def _(i):
         ct_start(dest(i))
 
-    start_own(1)
-    ct_start(z)
-    relay(0)
-
-    first_head = 3
+    relay_near(0)
+    relay_far(1)
+    start_own(2)
+
+    first_head = 4
     lag = 3
 
     @pl.loop(0, chunks)
@@ -375,21 +381,26 @@
             x_copies(k)[role].wait_recv()
         push(k)
 
+        @pl.when(k + 1 < chunks)
+        def _():
+            relay_near(k + 1)
+
         @pl.when(k + 2 < chunks)
         def _():
-            start_own(k + 2)
+            relay_far(k + 2)
+
+        @pl.when(k + 3 < chunks)
+        def _():
+            start_own(k + 3)
 
         @pl.when(k == 0)
         def _():
+            ct_start(z)
             att_start((0, 1))
 
         @pl.when(k == 1)
         def _():
             att_start((2, 3))
-
-        @pl.when(k + 1 < chunks)
-        def _():
-            relay(k + 1)
 
         @pl.when(k == first_head)
         def _():
@@ -496,7 +507,7 @@
             dma((nz, chunks)), dma((nz + 1, chunks)),
         ],
         compiler_params=pltpu.CompilerParams(
-            collective_id=0, has_side_effects=True, vmem_limit_bytes=60 * 1024 * 1024
+            collective_id=0, has_side_effects=True, vmem_limit_bytes=44 * 1024 * 1024
         ),
         name="fused",
     )(
@@ -511,7 +522,7 @@
     hidden, model = args[7].shape[3], args[6].shape[3]
     own = hidden // (members * groups)
     fits = members == 4 and near == 2 and groups % 2 == 0 and own % 16 == 0 and model % WIDTH == 0
-    if fits and model // WIDTH >= 3 + args[0].shape[3] // members // HEAD_DIM:
+    if fits and model // WIDTH >= 4 + args[0].shape[3] // members // HEAD_DIM:
         return fused_call(groups // near, *args)
     return per_device(*args)
 

time: 180 us -> 152 us (0.84); the launches traced: 179 us -> 149 us
  Pallas kernels: 165 us -> 135 us
    pallas_call x1, Pallas kernels: 165 us -> 135 us  [fused_call(): pl.pallas_call(functools.partial(fused_kernel, nz), out_shape=(jax.ShapeD...]
    unnamed x5 -> x15, local copies, waits for them, and re-layouts: 7.47 us -> 6.49 us
where the time goes in v2:
time: 152 us; the launch traced here: 149 us
  Pallas kernels  135 us (89%)
  local copies, waits for them, and re-layouts  9.14 us (6%)
  other arithmetic  4.63 us (3%)
    pallas_call x1, Pallas kernels, fused_call(): pl.pallas_call(functools.partial(fused_kernel, nz), out_shape=(jax.ShapeD...  135 us
    unnamed x15, local copies, waits for them, and re-layouts  6.49 us
    transpose x1, other arithmetic, fused_call(): ct = up_cot.T.reshape(members, groups, own, rows)  3.91 us

profile of v2, /device:TPU:0, one launch (start us, length us, event | category | flops | bytes accessed | tf_op | source)
XLA Modules:
  0.0 149.5 jit_solution(4539878651730350731)
XLA Ops:
  0.6 0.7 fusion.6
  1.3 0.1 and.22
  1.4 0.7 lt.23
  2.2 0.0 copy-start
  2.2 0.0 copy-start.1
  2.2 3.9 %fusion.5 = bf16[5632,128]{0,1:T(8,128)(2,1)} fusion(bf16[1,1,128,5632]{3,2,1,0:T(8,128)(2,1)} %param.16, bf16[1,1,128,5632]{3,2,1,0:T(8,128)(2,1)} %param.17), kind=kLoop, calls=%fused_computation.7 | loop fusion | flops 5767168 | bytes 4325376 | tf_op jit(solution)/shard_map/transpose | solution.py:477
  6.1 1.8 %copy.14 = bf16[5632,128]{1,0:T(8,128)(2,1)S(1)} copy(bf16[5632,128]{0,1:T(8,128)(2,1)} %fusion.5) | data formatting | bytes 2883584 | tf_op jit(solution)/shard_map/transpose | solution.py:477
  8.0 0.0 copy-done
  8.0 0.0 copy-done.1
  8.0 0.0 copy-start.2
  8.0 1.2 copy-done.2
  9.2 0.0 copy-start.3
  9.2 1.0 copy-done.3
  10.3 0.0 copy-start.4
  10.3 1.0 copy-done.4
  11.3 135.0 %fused.1 = (bf16[128,2048]{1,0:T(8,128)(2,1)S(1)}, bf16[128,2048]{1,0:T(8,128)(2,1)S(1)}, f32[176,4096]{1,0:T(8,128)S(1)}) custom-call(f32[4,1,1024]{2,1,0:T(1,128)S(1)} %and_convert_fusion.mask_ref, bf16[128,2048]{1,0:T(8,128)(2,1)S(1)} %bitcast.35, bf16[256,2048]{1,0:T(8,128)(2,1)S(1)} %bitcast.30, bf16[256,2048]{1,0:T(8,128)(2,1)S(1)} %bitcast.31, ...), custom_call_target="tpu_custom_call" | custom-call | tf_op jit(solution)/shard_map/fused/pallas_call | solution.py:483
  146.3 0.8 copy.19
  147.1 0.8 copy.20
  147.9 1.6 %copy.21 = f32[4096,176]{0,1:T(8,128)} copy(f32[4096,176]{0,1:T(8,128)S(1)} %bitcast.29) | data formatting | bytes 5767168
  (5 shorter events, 0.1 us)
Async XLA Ops:
  2.2 5.8 %copy-start = (bf16[1,1,256,2048]{3,2,1,0:T(8,128)(2,1)S(1)}, bf16[1,1,256,2048]{3,2,1,0:T(8,128)(2,1)}, u32[]{:S(2)}) copy-start(bf16[1,1,256,2048]{3,2,1,0:T(8,128)(2,1)} %param.10) | copy-start | bytes 3145732
  2.2 5.8 %copy-start.1 = (bf16[1,1,256,2048]{3,2,1,0:T(8,128)(2,1)S(1)}, bf16[1,1,256,2048]{3,2,1,0:T(8,128)(2,1)}, u32[]{:S(2)}) copy-start(bf16[1,1,256,2048]{3,2,1,0:T(8,128)(2,1)} %param.11) | copy-start | bytes 3145732
  8.0 1.2 copy-start.2
  9.2 1.0 copy-start.3
  10.3 1.0 copy-start.4

commit v3 on v2

--- a/solution.py
+++ b/solution.py
@@ -118,7 +118,7 @@
     mask_ref, q_ref, k_ref, v_ref, g_ref, x_ref, ct_ref,
     attn_ref, qgrad_ref, up_ref,
     xall, ctall, qb, kb, vb, gb, res, back, outgo, income,
-    x_send, x_recv, c_send, c_recv, a_send, a_recv, b_send, b_recv, z_send, z_recv,
+    x_send, x_recv, c_send, c_recv, a_send, a_recv, b_send, b_recv, z_send, z_recv, l_sem,
 ):
     grp = lax.axis_index("grp")
     dp = lax.axis_index("dp")
@@ -197,7 +197,6 @@
 
     def start_own(k):
         cs = x_copies(k)
-        cs[1].start()
         cs[0].start()
         cs[3].start()
 
@@ -350,16 +349,25 @@
 
     for t in range(nz):
         ctall[t, :, rows_of(mine)] = ct_ref[grp, t * 2 + x]
-    for k in range(chunks):
-        xall[k, rows_of(mine)] = x_ref[:, k * WIDTH : (k + 1) * WIDTH]
-    for src, dst in pairs:
-        dst[grp] = src[:, cols_of(grp, span)]
+    local = [
+        pltpu.make_async_copy(
+            x_ref.at[:, pl.ds(k * WIDTH, WIDTH)], xall.at[k, rows_of(mine)], l_sem.at[k]
+        )
+        for k in range(chunks)
+    ] + [
+        pltpu.make_async_copy(src.at[:, cols_of(grp, span)], dst.at[grp], l_sem.at[chunks + a])
+        for a, (src, dst) in enumerate(pairs)
+    ]
+    for copy in local:
+        copy.start()
 
     others = 7 + jnp.where(z > 0, 1, 0) + jnp.where(z < nz - 1, 1, 0)
     pl.semaphore_wait(barrier, others)
 
     ct_start(dest(0))
     start_own(0)
+    for k in range(2):
+        x_copies(k)[1].start()
     ct_start(dest(1))
     relay_far(0)
     start_own(1)
@@ -371,9 +379,15 @@
     relay_near(0)
     relay_far(1)
     start_own(2)
-
-    first_head = 4
-    lag = 3
+    for k in range(2, chunks):
+        x_copies(k)[1].start()
+
+    first_head = chunks // 2
+    per_step = pl.cdiv(heads, chunks - first_head)
+    lag = min(3, chunks - 2)
+
+    for copy in local:
+        copy.wait()
 
     @pl.loop(0, chunks)
     def _(k):
@@ -396,9 +410,13 @@
         @pl.when(k == 0)
         def _():
             ct_start(z)
+            pass
+
+        @pl.when(k == 1)
+        def _():
             att_start((0, 1))
 
-        @pl.when(k == 1)
+        @pl.when(k == 2)
         def _():
             att_start((2, 3))
 
@@ -408,9 +426,12 @@
                 for j in range(1, members):
                     att_copy(a, *pairs[a], j).wait_recv()
 
-        @pl.when(jnp.logical_and(k >= first_head, k < first_head + heads))
-        def _():
-            head(k - first_head)
+        for n in range(per_step):
+            h = (k - first_head) * per_step + n
+
+            @pl.when(jnp.logical_and(k >= first_head, h < heads))
+            def _(h=h):
+                head(h)
 
         @pl.when(k == lag)
         def _():
@@ -487,7 +508,7 @@
             jax.ShapeDtypeStruct((rows, width), BF16),
             jax.ShapeDtypeStruct((own, model), F32),
         ),
-        in_specs=[vm] * 7,
+        in_specs=[vm] + [pl.BlockSpec(memory_space=pltpu.HBM)] * 5 + [vm],
         out_specs=(vm, vm, vm),
         scratch_shapes=[
             pltpu.VMEM((chunks, layer * rows, WIDTH), BF16),
@@ -504,7 +525,7 @@
             dma((nz, 8)), dma((nz, 8)),
             dma((4, members)), dma((4, members)),
             dma((heads, 2, members)), dma((heads, 2, members)),
-            dma((nz, chunks)), dma((nz + 1, chunks)),
+            dma((nz, chunks)), dma((nz + 1, chunks)), dma((chunks + 4,)),
         ],
         compiler_params=pltpu.CompilerParams(
             collective_id=0, has_side_effects=True, vmem_limit_bytes=44 * 1024 * 1024
@@ -522,7 +543,7 @@
     hidden, model = args[7].shape[3], args[6].shape[3]
     own = hidden // (members * groups)
     fits = members == 4 and near == 2 and groups % 2 == 0 and own % 16 == 0 and model % WIDTH == 0
-    if fits and model // WIDTH >= 4 + args[0].shape[3] // members // HEAD_DIM:
+    if fits and model // WIDTH >= 4:
         return fused_call(groups // near, *args)
     return per_device(*args)
 

time: 152 us -> 143 us (0.941)
  Pallas kernels: 135 us -> 127 us
    pallas_call x1, Pallas kernels: 135 us -> 127 us  [fused_call(): pl.pallas_call(functools.partial(fused_kernel, nz), out_shape=(jax.ShapeD...]
where the time goes in v3:
time: 143 us; the launch traced here: 142 us
  Pallas kernels  127 us (89%)
  local copies, waits for them, and re-layouts  9.14 us (6%)
  other arithmetic  4.63 us (3%)
    pallas_call x1, Pallas kernels, fused_call(): pl.pallas_call(functools.partial(fused_kernel, nz), out_shape=(jax.ShapeD...  127 us
    unnamed x15, local copies, waits for them, and re-layouts  6.49 us
    transpose x1, other arithmetic, fused_call(): ct = up_cot.T.reshape(members, groups, own, rows)  3.91 us

profile of v3, /device:TPU:0, one launch (start us, length us, event | category | flops | bytes accessed | tf_op | source)
XLA Modules:
  0.0 141.8 jit_solution(7002262743994160217)
XLA Ops:
  0.6 0.7 fusion.6
  1.3 0.1 and.22
  1.4 0.7 lt.23
  2.2 0.0 copy-start
  2.2 0.0 copy-start.1
  2.2 3.9 %fusion.5 = bf16[5632,128]{0,1:T(8,128)(2,1)} fusion(bf16[1,1,128,5632]{3,2,1,0:T(8,128)(2,1)} %param.16, bf16[1,1,128,5632]{3,2,1,0:T(8,128)(2,1)} %param.17), kind=kLoop, calls=%fused_computation.7 | loop fusion | flops 5767168 | bytes 4325376 | tf_op jit(solution)/shard_map/transpose | solution.py:498
  6.1 1.8 %copy.14 = bf16[5632,128]{1,0:T(8,128)(2,1)S(1)} copy(bf16[5632,128]{0,1:T(8,128)(2,1)} %fusion.5) | data formatting | bytes 2883584 | tf_op jit(solution)/shard_map/transpose | solution.py:498
  8.0 0.0 copy-done
  8.0 0.0 copy-done.1
  8.0 0.0 copy-start.2
  8.0 1.2 copy-done.2
  9.2 0.0 copy-start.3
  9.2 1.0 copy-done.3
  10.3 0.0 copy-start.4
  10.3 1.0 copy-done.4
  11.3 127.3 %fused.1 = (bf16[128,2048]{1,0:T(8,128)(2,1)S(1)}, bf16[128,2048]{1,0:T(8,128)(2,1)S(1)}, f32[176,4096]{1,0:T(8,128)S(1)}) custom-call(f32[4,1,1024]{2,1,0:T(1,128)S(1)} %and_convert_fusion.mask_ref, bf16[128,2048]{1,0:T(8,128)(2,1)S(1)} %bitcast.35, bf16[256,2048]{1,0:T(8,128)(2,1)S(1)} %bitcast.30, bf16[256,2048]{1,0:T(8,128)(2,1)S(1)} %bitcast.31, ...), custom_call_target="tpu_custom_call" | custom-call | tf_op jit(solution)/shard_map/fused/pallas_call | solution.py:504
  138.6 0.8 copy.19
  139.4 0.8 copy.20
  140.2 1.6 %copy.21 = f32[4096,176]{0,1:T(8,128)} copy(f32[4096,176]{0,1:T(8,128)S(1)} %bitcast.29) | data formatting | bytes 5767168
  (5 shorter events, 0.1 us)
Async XLA Ops:
  2.2 5.8 %copy-start = (bf16[1,1,256,2048]{3,2,1,0:T(8,128)(2,1)S(1)}, bf16[1,1,256,2048]{3,2,1,0:T(8,128)(2,1)}, u32[]{:S(2)}) copy-start(bf16[1,1,256,2048]{3,2,1,0:T(8,128)(2,1)} %param.10) | copy-start | bytes 3145732
  2.2 5.8 %copy-start.1 = (bf16[1,1,256,2048]{3,2,1,0:T(8,128)(2,1)S(1)}, bf16[1,1,256,2048]{3,2,1,0:T(8,128)(2,1)}, u32[]{:S(2)}) copy-start(bf16[1,1,256,2048]{3,2,1,0:T(8,128)(2,1)} %param.11) | copy-start | bytes 3145732
  8.0 1.2 copy-start.2
  9.2 1.0 copy-start.3
  10.3 1.0 copy-start.4
